TPU v7x, 32 devices: a whole 2x2x4 slice. The times are simulated.
32 devices in a mesh: trial: 4 (over z), row: 8 (over y, x, core).
Axes of the slice: x: 2, y: 2, z: 4, core: 2. Of those that a mesh axis runs over, the one named last changes fastest.
Arguments:
- phase_map: float32 [4096, 512], P('row'), may hold values from -3.140625 to 3.140625
- target: float32 [4096, 512], P('row'), may hold values from 0 to 2
- distance: float32 [4], P('trial'), may hold values from 0.25 to 1
- etch_class: int32 [4, 32, 4], P('trial', 'row'), may hold values from 0 to 3
- class_offset: float32 [4], replicated, may hold values from -0.6 to 0.6
- aperture_start: int32 [4], replicated, may hold values from 0 to 7
- aperture_stop: int32 [4], replicated, may hold values from 25 to 32
Outputs:
- phase_grad: float32 [4096, 512], P('row', 'trial')
Inputs may be any that keep to these rules, and one draw needn't show every extreme that they name: `etch_class`: etch bias classes.
All inputs are finite; a program needn't handle non-finite values.
Results may differ from a plain program's by a relative error of at most 0.02.
Values may be sent and summed in bfloat16 or wider, within the bound.
A program may use at most 64 MiB of HBM per device.

v0:
```python
import jax
import jax.numpy as jnp
from jax import lax
from jax.sharding import PartitionSpec as P

BLK = 128


HIGHEST_PRECISION = lax.Precision.HIGHEST


def cosine_pair(numer, denom):
    angle = -2.0 * jnp.pi / denom * numer.astype(jnp.float32)
    return (jnp.cos(angle), jnp.sin(angle))


def column_tables(width, kept):
    columns = jnp.arange(width, dtype=jnp.int32)
    freqs = jnp.arange(kept, dtype=jnp.int32) - kept // 2
    table_real, table_imag = cosine_pair(jnp.mod(columns[:, None] * freqs[None, :], width), width)
    table_real = table_real.astype(jnp.bfloat16)
    table_imag = table_imag.astype(jnp.bfloat16)
    forward = jnp.concatenate(
        [
            jnp.concatenate([table_real, table_imag], 1),
            jnp.concatenate([-table_imag, table_real], 1),
        ],
        0,
    )
    backward = jnp.concatenate(
        [
            jnp.concatenate([table_real.T, -table_imag.T], 1),
            jnp.concatenate([table_imag.T, table_real.T], 1),
        ],
        0,
    )
    return (forward, backward)


def block_tables(height):
    places = jnp.arange(height, dtype=jnp.int32)
    table_real, table_imag = cosine_pair(jnp.mod(places[:, None] * places[None, :], height), height)
    table_real = table_real.astype(jnp.bfloat16)
    table_imag = table_imag.astype(jnp.bfloat16)
    forward = jnp.concatenate(
        [
            jnp.concatenate([table_real, -table_imag], 1),
            jnp.concatenate([table_imag, table_real], 1),
        ],
        0,
    )
    backward = jnp.concatenate(
        [
            jnp.concatenate([table_real, table_imag], 1),
            jnp.concatenate([-table_imag, table_real], 1),
        ],
        0,
    )
    return (forward, backward)


def transfer_phase(signed, across, dist, global_rows, width):
    row_freq = signed.astype(jnp.float32)
    col_freq = across.astype(jnp.float32)
    theta = (
        -jnp.pi
        * dist
        * (
            row_freq * row_freq * (1.0 / global_rows)
            + col_freq * col_freq * (global_rows / (width * width))
        )
    )
    return (jnp.cos(theta), jnp.sin(theta))


def small_einsum(form, table, values):
    return jnp.einsum(form, table, values, precision=HIGHEST_PRECISION)


def local(phase_map, target, distance, etch_class, class_offset, aperture_start, aperture_stop):
    height, width = phase_map.shape
    kept = width // 2
    groups = lax.axis_size("row")
    device = lax.axis_index("row")
    global_rows = height * groups
    slim_cols = kept // groups
    col_fwd, col_back = column_tables(width, kept)
    blk_fwd, blk_back = block_tables(height)
    group_ids = jnp.arange(groups, dtype=jnp.int32)
    small_real, small_imag = cosine_pair(
        jnp.mod(group_ids[:, None] * group_ids[None, :], groups), groups
    )
    local_rows = jnp.arange(height, dtype=jnp.int32)
    dist = distance[0]
    classes = etch_class[0]
    row_blocks, col_blocks = classes.shape
    levels = jnp.arange(class_offset.shape[0], dtype=jnp.int32)
    offsets = jnp.sum(jnp.where(classes[:, :, None] == levels, class_offset, 0.0), axis=2)
    offset_map = jnp.broadcast_to(
        offsets[:, None, :, None], (row_blocks, BLK, col_blocks, BLK)
    ).reshape(height, width)
    row_block = (device * height + local_rows) // BLK
    first_block = jnp.broadcast_to(aperture_start[:, None], (col_blocks, BLK)).reshape(width)
    stop_block = jnp.broadcast_to(aperture_stop[:, None], (col_blocks, BLK)).reshape(width)
    inside = (row_block[:, None] >= first_block[None, :]) & (
        row_block[:, None] < stop_block[None, :]
    )
    aperture_mask = inside.astype(jnp.float32)
    angle_map = phase_map + offset_map
    lens_real = aperture_mask * jnp.cos(angle_map)
    lens_imag = aperture_mask * jnp.sin(angle_map)
    twist_cols_real, twist_cols_imag = cosine_pair(
        jnp.mod(group_ids[:, None] * local_rows[None, :], global_rows), global_rows
    )
    twist_cols_real = twist_cols_real[None]
    twist_cols_imag = twist_cols_imag[None]

    def forward_columns(cols_real, cols_imag):
        parts = (
            lax.all_to_all(cols_real, "row", split_axis=0, concat_axis=1, tiled=True),
            lax.all_to_all(cols_imag, "row", split_axis=0, concat_axis=1, tiled=True),
        )
        part_real = parts[0].reshape(slim_cols, groups, height).astype(jnp.float32)
        part_imag = parts[1].reshape(slim_cols, groups, height).astype(jnp.float32)
        mixed_real = small_einsum("kp,cpl->ckl", small_real, part_real) - small_einsum(
            "kp,cpl->ckl", small_imag, part_imag
        )
        mixed_imag = small_einsum("kp,cpl->ckl", small_real, part_imag) + small_einsum(
            "kp,cpl->ckl", small_imag, part_real
        )
        turned_real = (mixed_real * twist_cols_real - mixed_imag * twist_cols_imag).astype(
            jnp.bfloat16
        )
        turned_imag = (mixed_real * twist_cols_imag + mixed_imag * twist_cols_real).astype(
            jnp.bfloat16
        )
        stacked = jnp.concatenate([turned_real, turned_imag], 2)
        spectrum = jnp.einsum("ckl,ol->cko", stacked, blk_fwd, preferred_element_type=jnp.float32)
        return (spectrum[:, :, :height], spectrum[:, :, height:])

    def inverse_columns(filtered_real, filtered_imag):
        stacked = jnp.concatenate([filtered_real, filtered_imag], 2)
        unmixed = jnp.einsum("ckl,ol->cko", stacked, blk_back, preferred_element_type=jnp.float32)
        unmixed_real = unmixed[:, :, :height]
        unmixed_imag = unmixed[:, :, height:]
        returned_real = (
            (unmixed_real * twist_cols_real + unmixed_imag * twist_cols_imag)
            .astype(jnp.bfloat16)
            .astype(jnp.float32)
        )
        returned_imag = (
            (unmixed_imag * twist_cols_real - unmixed_real * twist_cols_imag)
            .astype(jnp.bfloat16)
            .astype(jnp.float32)
        )
        near_real = (
            small_einsum("kp,ckl->cpl", small_real, returned_real)
            + small_einsum("kp,ckl->cpl", small_imag, returned_imag)
        ) * (1.0 / global_rows)
        near_imag = (
            small_einsum("kp,ckl->cpl", small_real, returned_imag)
            - small_einsum("kp,ckl->cpl", small_imag, returned_real)
        ) * (1.0 / global_rows)
        near_real = near_real.astype(jnp.bfloat16).reshape(slim_cols, global_rows)
        near_imag = near_imag.astype(jnp.bfloat16).reshape(slim_cols, global_rows)
        owned = (
            lax.all_to_all(near_real, "row", split_axis=1, concat_axis=0, tiled=True),
            lax.all_to_all(near_imag, "row", split_axis=1, concat_axis=0, tiled=True),
        )
        return (owned[0], owned[1])

    freq_rows = group_ids[None, :, None] + groups * local_rows[None, None, :]
    across = (device * slim_cols + jnp.arange(slim_cols, dtype=jnp.int32) - kept // 2)[
        :, None, None
    ]
    signed = jnp.mod(freq_rows + global_rows // 2, global_rows) - global_rows // 2
    filter_real, filter_imag = transfer_phase(signed, across, dist, global_rows, width)

    def propagate(field_real, field_imag, phase_real, phase_imag):
        stacked_field = jnp.concatenate([field_real, field_imag], 1)
        flipped = jnp.einsum(
            "rc,cj->jr", stacked_field, col_fwd, preferred_element_type=jnp.float32
        ).astype(jnp.bfloat16)
        spec_real, spec_imag = forward_columns(flipped[:kept], flipped[kept:])
        filtered_real = (spec_real * phase_real - spec_imag * phase_imag).astype(jnp.bfloat16)
        filtered_imag = (spec_real * phase_imag + spec_imag * phase_real).astype(jnp.bfloat16)
        near_real, near_imag = inverse_columns(filtered_real, filtered_imag)
        result = jnp.einsum(
            "jr,jo->ro",
            jnp.concatenate([near_real, near_imag], 0),
            col_back,
            preferred_element_type=jnp.float32,
        ) * (1.0 / width)
        return (result[:, :width], result[:, width:])

    focal_real, focal_imag = propagate(
        lens_real.astype(jnp.bfloat16), lens_imag.astype(jnp.bfloat16), filter_real, filter_imag
    )
    residual = focal_real * focal_real + focal_imag * focal_imag - target
    back_real, back_imag = propagate(
        (residual * focal_real).astype(jnp.bfloat16),
        (residual * focal_imag).astype(jnp.bfloat16),
        filter_real,
        -filter_imag,
    )
    gradient = 2.0 * (lens_real * back_imag - lens_imag * back_real)
    return lax.psum_scatter(
        gradient.astype(jnp.bfloat16), "trial", scatter_dimension=1, tiled=True
    ).astype(jnp.float32)


def solution(mesh):
    return jax.shard_map(
        local,
        mesh=mesh,
        in_specs=(
            P("row", None),
            P("row", None),
            P("trial"),
            P("trial", "row", None),
            P(),
            P(),
            P(),
        ),
        out_specs=P("row", "trial"),
        check_vma=False,
    )
```

profile of v0, /device:TPU:0, one launch (start us, length us, event | category | flops | bytes accessed | tf_op | source)
XLA Modules:
  0.0 170.8 jit_solution(2126734685454798621)
XLA Ops:
  6.5 2.0 %fusion.99 = bf16[512,256]{1,0:T(8,128)(2,1)S(1)} fusion(s32[256]{0:T(256)S(1)} %iota_add_fusion.1), kind=kLoop, calls=%fused_computation.150 | loop fusion | flops 2359296 | bytes 263168 | tf_op jit(solution)/shard_map/neg | solution.py:26
  8.6 2.2 %sine_convert_fusion.2 = (bf16[512,256]{1,0:T(8,128)(2,1)S(1)}, bf16[512,256]{1,0:T(8,128)(2,1)S(1)}) fusion(s32[256]{0:T(256)S(1)} %iota_add_fusion.1), kind=kLoop, calls=%fused_computation.123 | loop fusion | flops 2097152 | bytes 525312 | tf_op jit(solution)/shard_map/convert_element_type | solution.py:22
  10.8 0.9 select_reduce_fusion
  11.8 0.7 broadcast_bitcast_fusion
  12.5 0.2 broadcast_in_dim.18
  12.7 4.2 %fusion.43 = (bf16[512,512]{1,0:T(8,128)(2,1)S(1)}, bf16[512,512]{1,0:T(8,128)(2,1)S(1)}) fusion(s32[512]{0:T(512)S(1)} %get-tuple-element.29, s32[512]{0:T(512)S(1)} %get-tuple-element.30, s32[512]{0:T(512)S(1)} %add_select_fusion.6, f32[512,512]{1,0:T(8,128)S(1)} %copy-done, f32[64,8,4,128]{3,2,1,0:T(4,128)S(1)} %bitcast.136), kind=kLoop, calls=%fused_computation.77 | loop fusion | flops 2097152 | bytes 3151872 | tf_op jit(solution)/shard_map/convert_element_type | solution.py:197
  17.0 0.8 convolution_convert_fusion.1
  17.7 0.8 fusion.234
  18.6 5.2 %all-to-all-start = ((bf16[8,32,512]{2,1,0:T(8,128)(2,1)}), bf16[8,32,512]{2,1,0:T(8,128)(2,1)S(1)}, u32[]{:S(2)}, u32[]{:S(2)}) async-start(bf16[8,32,512]{2,1,0:T(8,128)(2,1)} %bitcast.3), calls=%async_computation | async-start | bytes 524288 | tf_op jit(solution)/shard_map/all_to_all | solution.py:120
  23.9 4.6 %fusion.98 = bf16[512,512]{1,0:T(8,128)(2,1)} fusion(), kind=kLoop, calls=%fused_computation.149 | loop fusion | flops 4718592 | bytes 524288 | tf_op jit(solution)/shard_map/neg | solution.py:47
  28.5 4.6 %cosine_convert_fusion = bf16[512,512]{1,0:T(8,128)(2,1)} fusion(), kind=kLoop, calls=%fused_computation.64 | loop fusion | flops 3932160 | bytes 524288 | tf_op jit(solution)/shard_map/convert_element_type | solution.py:43
  33.1 4.6 %sine_convert_fusion = bf16[512,512]{1,0:T(8,128)(2,1)} fusion(), kind=kLoop, calls=%fused_computation.63 | loop fusion | flops 3932160 | bytes 524288 | tf_op jit(solution)/shard_map/convert_element_type | solution.py:44
  37.7 3.1 %sine_convert_fusion.1 = (bf16[256,512]{1,0:T(8,128)(2,1)S(1)}, bf16[256,512]{1,0:T(8,128)(2,1)}) fusion(s32[256]{0:T(256)S(1)} %iota_add_fusion.1), kind=kLoop, calls=%fused_computation.109 | loop fusion | flops 2097152 | bytes 525312 | tf_op jit(solution)/shard_map/convert_element_type | solution.py:22
  41.5 4.2 %all-to-all-start.1 = ((bf16[8,32,512]{2,1,0:T(8,128)(2,1)}), bf16[8,32,512]{2,1,0:T(8,128)(2,1)S(1)}, u32[]{:S(2)}, u32[]{:S(2)}) async-start(bf16[8,32,512]{2,1,0:T(8,128)(2,1)} %bitcast.6), calls=%async_computation.1 | async-start | bytes 524288 | tf_op jit(solution)/shard_map/all_to_all | solution.py:121
  45.7 0.5 fusion.88
  46.2 6.4 %all-to-all-done.1 = bf16[8,32,512]{2,1,0:T(8,128)(2,1)S(1)} async-done(((bf16[8,32,512]{2,1,0:T(8,128)(2,1)}), bf16[8,32,512]{2,1,0:T(8,128)(2,1)S(1)}, u32[]{:S(2)}, u32[]{:S(2)}) %all-to-all-start.1) | async-done | bytes 262176 | tf_op jit(solution)/shard_map/all_to_all | solution.py:121
  52.6 0.5 fusion.84
  53.1 0.5 fusion.15
  53.6 0.6 subtract_convert_fusion.5
  54.3 0.7 fusion.10
  55.0 2.3 %subtract_convert_fusion.4 = (bf16[32,8,512]{2,1,0:T(8,128)(2,1)S(1)}, bf16[32,8,512]{2,1,0:T(8,128)(2,1)S(1)}) fusion(f32[32,8,1024]{2,1,0:T(8,128)S(1)} %fusion.10, f32[32]{0:T(128)S(1)} %multiply_multiply_fusion, f32[8,512]{1,0:T(8,128)S(1)} %fusion.108, f32[]{:T(128)} %bitcast.14), kind=kLoop, calls=%fused_computation.116 | loop fusion | flops 1310720 | bytes 1589380 | tf_op jit(solution)/shard_map/convert_element_type | solution.py:185
  57.4 0.8 fusion.6
  58.1 0.2 add_convert_fusion.3
  58.3 0.4 fusion.133
  58.7 0.4 fusion.131
  59.1 0.4 fusion.24
  59.6 0.8 copy.58
  60.4 4.1 %all-to-all-start.2 = ((bf16[32,8,512]{2,0,1:T(8,128)(2,1)}), bf16[32,8,512]{2,0,1:T(8,128)(2,1)}, u32[]{:S(2)}, u32[]{:S(2)}) async-start(bf16[32,8,512]{2,0,1:T(8,128)(2,1)} %copy.58), calls=%async_computation.2 | async-start | bytes 524288 | tf_op jit(solution)/shard_map/all_to_all | solution.py:167
  64.4 0.4 fusion.25
  64.9 0.8 copy.59
  65.6 5.7 %all-to-all-done.2 = bf16[32,8,512]{2,0,1:T(8,128)(2,1)} async-done(((bf16[32,8,512]{2,0,1:T(8,128)(2,1)}), bf16[32,8,512]{2,0,1:T(8,128)(2,1)}, u32[]{:S(2)}, u32[]{:S(2)}) %all-to-all-start.2) | async-done | bytes 262176 | tf_op jit(solution)/shard_map/all_to_all | solution.py:167
  71.4 3.4 %all-to-all-start.3 = ((bf16[32,8,512]{2,0,1:T(8,128)(2,1)}), bf16[32,8,512]{2,0,1:T(8,128)(2,1)S(1)}, u32[]{:S(2)}, u32[]{:S(2)}) async-start(bf16[32,8,512]{2,0,1:T(8,128)(2,1)} %copy.59), calls=%async_computation.3 | async-start | bytes 524288 | tf_op jit(solution)/shard_map/all_to_all | solution.py:168
  74.8 2.2 %fusion.100 = bf16[256,512]{1,0:T(8,128)(2,1)S(1)} fusion(s32[256]{0:T(256)S(1)} %iota_add_fusion.1), kind=kLoop, calls=%fused_computation.151 | loop fusion | flops 2359296 | bytes 263168 | tf_op jit(solution)/shard_map/neg | solution.py:32
  77.0 4.7 %all-to-all-done.3 = bf16[32,8,512]{2,0,1:T(8,128)(2,1)S(1)} async-done(((bf16[32,8,512]{2,0,1:T(8,128)(2,1)}), bf16[32,8,512]{2,0,1:T(8,128)(2,1)S(1)}, u32[]{:S(2)}, u32[]{:S(2)}) %all-to-all-start.3) | async-done | bytes 262176 | tf_op jit(solution)/shard_map/all_to_all | solution.py:168
  81.6 1.8 %convolution_multiply_fusion.1 = f32[512,1024]{1,0:T(8,128)S(1)} fusion(bf16[256,512]{1,0:T(8,128)(2,1)S(1)} %bitcast.140, bf16[256,512]{1,0:T(8,128)(2,1)} %bitcast.20, bf16[256,512]{1,0:T(8,128)(2,1)S(1)} %copy-done.8, bf16[256,512]{1,0:T(8,128)(2,1)S(1)} %get-tuple-element.25, bf16[256,512]{1,0:T(8,128)(2,1)S(1)} %fusion.100), kind=kOutput, calls=%fused_computation.9 | convolution fusion | flops 542638080 | bytes 3407872 | tf_op jit(solution)/shard_map/jr,jo->ro/dot_general | solution.py:188
  83.4 0.4 multiply_convert_fusion.1
  83.9 0.5 copy-done.11
  84.5 0.8 convolution_convert_fusion
  85.3 0.7 fusion.233
  86.0 9.3 %all_to_all.128 = bf16[8,32,512]{2,1,0:T(8,128)(2,1)S(1)} all-to-all(bf16[8,32,512]{2,1,0:T(8,128)(2,1)S(1)} %bitcast.139), channel_id=1, replica_groups=mesh['trial'=4,'row'=8] {'row'}, dimensions={0} | all-to-all | bytes 524288 | tf_op jit(solution)/shard_map/all_to_all | solution.py:120
  95.3 3.6 %all-to-all-start.5 = ((bf16[8,32,512]{2,1,0:T(8,128)(2,1)}), bf16[8,32,512]{2,1,0:T(8,128)(2,1)S(1)}, u32[]{:S(2)}, u32[]{:S(2)}) async-start(bf16[8,32,512]{2,1,0:T(8,128)(2,1)} %bitcast.27), calls=%async_computation.5 | async-start | bytes 524288 | tf_op jit(solution)/shard_map/all_to_all | solution.py:121
  99.0 0.5 fusion.82
  99.5 6.1 %all-to-all-done.5 = bf16[8,32,512]{2,1,0:T(8,128)(2,1)S(1)} async-done(((bf16[8,32,512]{2,1,0:T(8,128)(2,1)}), bf16[8,32,512]{2,1,0:T(8,128)(2,1)S(1)}, u32[]{:S(2)}, u32[]{:S(2)}) %all-to-all-start.5) | async-done | bytes 262176 | tf_op jit(solution)/shard_map/all_to_all | solution.py:121
  105.6 0.5 fusion.78
  106.1 0.5 fusion.13
  106.6 0.6 subtract_convert_fusion.2
  107.3 0.8 fusion.8
  108.1 2.4 %subtract_convert_fusion.1 = (bf16[32,8,512]{2,1,0:T(8,128)(2,1)S(1)}, bf16[32,8,512]{2,1,0:T(8,128)(2,1)S(1)}) fusion(f32[32,8,1024]{2,1,0:T(8,128)S(1)} %fusion.8, f32[32]{0:T(128)S(1)} %multiply_multiply_fusion, f32[8,512]{1,0:T(8,128)S(1)} %fusion.108, f32[]{:T(128)} %bitcast.14), kind=kLoop, calls=%fused_computation.106 | loop fusion | flops 1441792 | bytes 1589380 | tf_op jit(solution)/shard_map/convert_element_type | solution.py:185
  110.4 0.8 fusion.4
  111.2 0.2 add_convert_fusion
  111.3 0.4 fusion.129
  111.8 0.4 fusion.127
  112.2 0.4 fusion.26
  112.6 0.8 copy.66
  113.4 4.0 %all-to-all-start.6 = ((bf16[32,8,512]{2,0,1:T(8,128)(2,1)}), bf16[32,8,512]{2,0,1:T(8,128)(2,1)}, u32[]{:S(2)}, u32[]{:S(2)}) async-start(bf16[32,8,512]{2,0,1:T(8,128)(2,1)} %copy.66), calls=%async_computation.6 | async-start | bytes 524288 | tf_op jit(solution)/shard_map/all_to_all | solution.py:167
  117.5 0.4 fusion.27
  118.0 6.3 %all-to-all-done.6 = bf16[32,8,512]{2,0,1:T(8,128)(2,1)} async-done(((bf16[32,8,512]{2,0,1:T(8,128)(2,1)}), bf16[32,8,512]{2,0,1:T(8,128)(2,1)}, u32[]{:S(2)}, u32[]{:S(2)}) %all-to-all-start.6) | async-done | bytes 262176 | tf_op jit(solution)/shard_map/all_to_all | solution.py:167
  124.4 9.3 %all_to_all.129 = bf16[32,8,512]{2,0,1:T(8,128)(2,1)S(1)} all-to-all(bf16[32,8,512]{2,0,1:T(8,128)(2,1)S(1)} %copy.67), channel_id=1, replica_groups=mesh['trial'=4,'row'=8] {'row'}, dimensions={1} | all-to-all | bytes 524288 | tf_op jit(solution)/shard_map/all_to_all | solution.py:168
  133.7 1.8 %convolution_multiply_fusion = f32[512,1024]{1,0:T(8,128)S(1)} fusion(bf16[256,512]{1,0:T(8,128)(2,1)S(1)} %bitcast.141, bf16[256,512]{1,0:T(8,128)(2,1)} %bitcast.36, bf16[256,512]{1,0:T(8,128)(2,1)S(1)} %copy-done.9, bf16[256,512]{1,0:T(8,128)(2,1)S(1)} %get-tuple-element.25, bf16[256,512]{1,0:T(8,128)(2,1)} %copy-done.16), kind=kOutput, calls=%fused_computation.8 | convolution fusion | flops 542638080 | bytes 3407872 | tf_op jit(solution)/shard_map/jr,jo->ro/dot_general | solution.py:188
  135.5 4.3 %fusion.33 = bf16[512,512]{1,0:T(8,128)(2,1)S(1)} fusion(f32[512,1024]{1,0:T(8,128)S(1)} %convolution_multiply_fusion, s32[512]{0:T(512)S(1)} %get-tuple-element.29, s32[512]{0:T(512)S(1)} %get-tuple-element.30, s32[512]{0:T(512)S(1)} %add_select_fusion.6, f32[512,512]{1,0:T(8,128)S(1)} %copy-done, f32[64,8,4,128]{3,2,1,0:T(4,128)S(1)} %bitcast.137), kind=kLoop, calls=%fused_computation.50 | loop fusion | flops 2883584 | bytes 4724736 | tf_op jit(solution)/shard_map/convert_element_type | solution.py:208
  139.8 1.0 copy.84
  140.9 21.4 %reduce-scatter.4.cloned.1.call-done = bf16[128,512]{1,0:T(8,128)(2,1)} async-done(((bf16[512,512]{1,0:T(8,128)(2,1)}), bf16[128,512]{1,0:T(8,128)(2,1)}) %reduce-scatter.4.cloned.1.call-update) | async-done | bytes 131088
  162.2 1.0 copy.85
  163.2 0.7 convert_element_type.296
  (43 shorter events, 0.5 us)
Async XLA Ops:
  6.5 6.2 %copy-start = (f32[512,512]{1,0:T(8,128)S(1)}, f32[512,512]{1,0:T(8,128)}, u32[]{:S(2)}) copy-start(f32[512,512]{1,0:T(8,128)} %param.7) | copy-start | bytes 3145732
  8.6 8.4 %copy-start.10 = (bf16[512,256]{1,0:T(8,128)(2,1)}, bf16[512,256]{1,0:T(8,128)(2,1)S(1)}, u32[]{:S(2)}) copy-start(bf16[512,256]{1,0:T(8,128)(2,1)S(1)} %fusion.99) | copy-start | bytes 786436
  10.8 6.2 %copy-start.12 = (bf16[512,256]{1,0:T(8,128)(2,1)}, bf16[512,256]{1,0:T(8,128)(2,1)S(1)}, u32[]{:S(2)}) copy-start(bf16[512,256]{1,0:T(8,128)(2,1)S(1)} %get-tuple-element.27) | copy-start | bytes 786436
  10.8 6.2 %copy-start.14 = (bf16[512,256]{1,0:T(8,128)(2,1)}, bf16[512,256]{1,0:T(8,128)(2,1)S(1)}, u32[]{:S(2)}) copy-start(bf16[512,256]{1,0:T(8,128)(2,1)S(1)} %get-tuple-element.28) | copy-start | bytes 786436
  18.6 22.9 %all-to-all-start = ((bf16[8,32,512]{2,1,0:T(8,128)(2,1)}), bf16[8,32,512]{2,1,0:T(8,128)(2,1)S(1)}, u32[]{:S(2)}, u32[]{:S(2)}) async-start(bf16[8,32,512]{2,1,0:T(8,128)(2,1)} %bitcast.3), calls=%async_computation | async-start | bytes 524288 | tf_op jit(solution)/shard_map/all_to_all | solution.py:120
  41.5 11.1 %all-to-all-start.1 = ((bf16[8,32,512]{2,1,0:T(8,128)(2,1)}), bf16[8,32,512]{2,1,0:T(8,128)(2,1)S(1)}, u32[]{:S(2)}, u32[]{:S(2)}) async-start(bf16[8,32,512]{2,1,0:T(8,128)(2,1)} %bitcast.6), calls=%async_computation.1 | async-start | bytes 524288 | tf_op jit(solution)/shard_map/all_to_all | solution.py:121
  52.6 1.7 copy-start.2
  52.6 1.7 copy-start.4
  52.6 1.7 copy-start.6
  59.1 22.5 %copy-start.8 = (bf16[256,512]{1,0:T(8,128)(2,1)S(1)}, bf16[256,512]{1,0:T(8,128)(2,1)}, u32[]{:S(2)}) copy-start(bf16[256,512]{1,0:T(8,128)(2,1)} %get-tuple-element.26) | copy-start | bytes 786436
  60.4 11.0 %all-to-all-start.2 = ((bf16[32,8,512]{2,0,1:T(8,128)(2,1)}), bf16[32,8,512]{2,0,1:T(8,128)(2,1)}, u32[]{:S(2)}, u32[]{:S(2)}) async-start(bf16[32,8,512]{2,0,1:T(8,128)(2,1)} %copy.58), calls=%async_computation.2 | async-start | bytes 524288 | tf_op jit(solution)/shard_map/all_to_all | solution.py:167
  71.4 10.3 %all-to-all-start.3 = ((bf16[32,8,512]{2,0,1:T(8,128)(2,1)}), bf16[32,8,512]{2,0,1:T(8,128)(2,1)S(1)}, u32[]{:S(2)}, u32[]{:S(2)}) async-start(bf16[32,8,512]{2,0,1:T(8,128)(2,1)} %copy.59), calls=%async_computation.3 | async-start | bytes 524288 | tf_op jit(solution)/shard_map/all_to_all | solution.py:168
  76.9 8.3 %copy-start.16 = (bf16[256,512]{1,0:T(8,128)(2,1)}, bf16[256,512]{1,0:T(8,128)(2,1)S(1)}, u32[]{:S(2)}) copy-start(bf16[256,512]{1,0:T(8,128)(2,1)S(1)} %fusion.100) | copy-start | bytes 786436
  81.6 1.8 %copy-start.1 = (f32[512,512]{1,0:T(8,128)S(1)}, f32[512,512]{1,0:T(8,128)}, u32[]{:S(2)}) copy-start(f32[512,512]{1,0:T(8,128)} %param.8) | copy-start | bytes 3145732
  83.4 1.0 copy-start.11
  83.4 1.0 copy-start.13
  83.4 1.1 copy-start.15
  95.3 10.3 %all-to-all-start.5 = ((bf16[8,32,512]{2,1,0:T(8,128)(2,1)}), bf16[8,32,512]{2,1,0:T(8,128)(2,1)S(1)}, u32[]{:S(2)}, u32[]{:S(2)}) async-start(bf16[8,32,512]{2,1,0:T(8,128)(2,1)} %bitcast.27), calls=%async_computation.5 | async-start | bytes 524288 | tf_op jit(solution)/shard_map/all_to_all | solution.py:121
  105.6 1.7 copy-start.3
  105.6 1.7 copy-start.5
  105.6 1.7 copy-start.7
  112.2 21.5 %copy-start.9 = (bf16[256,512]{1,0:T(8,128)(2,1)S(1)}, bf16[256,512]{1,0:T(8,128)(2,1)}, u32[]{:S(2)}) copy-start(bf16[256,512]{1,0:T(8,128)(2,1)} %get-tuple-element.26) | copy-start | bytes 786436
  113.4 11.0 %all-to-all-start.6 = ((bf16[32,8,512]{2,0,1:T(8,128)(2,1)}), bf16[32,8,512]{2,0,1:T(8,128)(2,1)}, u32[]{:S(2)}, u32[]{:S(2)}) async-start(bf16[32,8,512]{2,0,1:T(8,128)(2,1)} %copy.66), calls=%async_computation.6 | async-start | bytes 524288 | tf_op jit(solution)/shard_map/all_to_all | solution.py:167
  117.5 44.7 %reduce-scatter.4.cloned.1.call-start = ((), (), s32[]{:S(2)}) async-start(), calls=%async_computation.9 | async-start | bytes 655360
Sparse Core Ops, SparseCore 0:
  141.0 21.1 reduce-scatter.3
where the time goes:
time: 172 us; the launch traced here: 171 us
  waiting for transfers between devices  50.6 us (29%)
  other arithmetic  39.1 us (23%)
  starting transfers between devices  24.6 us (14%)
  blocking collectives  18.6 us (11%)
  matrix products  15.7 us (9%)
  between operations  14.6 us (8%)
  local copies, waits for them, and re-layouts  7.68 us (4%)
    unnamed x2, waiting for transfers between devices  21.4 us
    all_to_all x2, waiting for transfers between devices, forward_columns(): lax.all_to_all(cols_imag, 'row', split_axis=0, concat_axis=1, tiled=True)  12.5 us
    all_to_all x2, waiting for transfers between devices, inverse_columns(): lax.all_to_all(near_real, 'row', split_axis=1, concat_axis=0, tiled=True)  12.1 us
    all_to_all x1, blocking collectives, inverse_columns(): lax.all_to_all(near_imag, 'row', split_axis=1, concat_axis=0, tiled=True)  9.3 us
    all_to_all x1, blocking collectives, forward_columns(): lax.all_to_all(cols_real, 'row', split_axis=0, concat_axis=1, tiled=True)  9.3 us
    all_to_all x2, starting transfers between devices, inverse_columns(): lax.all_to_all(near_real, 'row', split_axis=1, concat_axis=0, tiled=True)  8.1 us
    all_to_all x2, starting transfers between devices, forward_columns(): lax.all_to_all(cols_imag, 'row', split_axis=0, concat_axis=1, tiled=True)  7.84 us
    dot_general x16, matrix products, small_einsum(): return jnp.einsum(form, table, values, precision=HIGHEST_PRECISION)  7.7 us
  transfers between devices with their start and end apart: 7, of which 6 were waited for; matrix products, arithmetic and copies ran while one was open for 13% of the time, Pallas kernels for 0%

commit v1 on v0

v1 whole, which is shorter than its diff:
```python
import math

import jax
import jax.numpy as jnp
import numpy as np
from jax import lax
from jax.experimental import pallas as pl
from jax.experimental.pallas import tpu as pltpu
from jax.sharding import PartitionSpec as P

BLK = 128
LANES = 128
F32 = jnp.float32
BF16 = jnp.bfloat16
MESH = pl.DeviceIdType.MESH
MAGIC = 12582912.0


def even_fit(func, degree):
    cheb = np.polynomial.chebyshev.Chebyshev.interpolate(func, degree, domain=[0.0, 0.25])
    return [float(c) for c in cheb.convert(kind=np.polynomial.Polynomial).coef]


COS_FIT = even_fit(lambda z: np.cos(np.pi * np.sqrt(z)), 6)
SIN_FIT = even_fit(lambda z: np.pi * np.sinc(np.sqrt(z)), 5)


def horner(coefs, z):
    total = jnp.full_like(z, coefs[-1])
    for c in coefs[-2::-1]:
        total = total * z + c
    return total


def nearest(u):
    return (u + MAGIC) - MAGIC


def turn(u):
    whole = nearest(u)
    rest = u - whole
    z = rest * rest
    return horner(COS_FIT, z), rest * horner(SIN_FIT, z), whole


def cos_sin_pi(u):
    cos, sin, whole = turn(u)
    half = whole * 0.5
    odd = half - nearest(half)
    sign = 1.0 - 8.0 * (odd * odd)
    return cos * sign, sin * sign


def scale_turn(re, im, k, n, sign):
    if k == 0:
        return re, im
    if 4 * k == n:
        return (-im, re) if sign > 0 else (im, -re)
    c = math.cos(2 * math.pi * k / n)
    s = sign * math.sin(2 * math.pi * k / n)
    if 8 * k == n:
        return ((re - im) * c, (re + im) * c) if sign > 0 else ((re + im) * c, (im - re) * c)
    return re * c - im * s, re * s + im * c


def small_dft(values, sign):
    n = len(values)
    if n == 1:
        return values
    even = small_dft(values[0::2], sign)
    odd = small_dft(values[1::2], sign)
    low, high = [], []
    for k in range(n // 2):
        re, im = scale_turn(*odd[k], k, n, sign)
        low.append((even[k][0] + re, even[k][1] + im))
        high.append((even[k][0] - re, even[k][1] - im))
    return low + high


def tables(height, width, kept, groups, chunks):
    slim = kept // groups
    part = slim // chunks
    cols = np.arange(width)
    freqs = np.arange(kept) - kept // 2
    angle = -2.0 * np.pi / width * np.mod(cols[:, None] * freqs[None, :], width)
    re = np.cos(angle).T.reshape(groups, chunks, part, width)
    im = np.sin(angle).T.reshape(groups, chunks, part, width)
    rows_re = np.concatenate([re, -im], 3)
    rows_im = np.concatenate([im, re], 3)
    forward = np.stack([rows_re, rows_im], 2)
    forward = forward.transpose(1, 0, 2, 3, 4).reshape(2 * kept, 2 * width)
    places = np.arange(height)
    angle = -2.0 * np.pi / height * np.mod(places[:, None] * places[None, :], height)
    blk = np.stack([np.cos(angle), np.sin(angle)])
    total = height * groups
    angle = -2.0 * np.pi / total * np.mod(np.arange(groups)[:, None] * places[None, :], total)
    twist = np.stack([np.cos(angle), np.sin(angle)])
    as_bf16 = lambda a: jnp.asarray(a.astype(np.float32).astype(BF16))
    return as_bf16(forward), as_bf16(forward.T), as_bf16(blk), jnp.asarray(twist.astype(np.float32))


def kernel(
    dims,
    dist_ref,
    class_ref,
    level_ref,
    start_ref,
    stop_ref,
    phase_ref,
    target_ref,
    fwd_ref,
    back_ref,
    blk_ref,
    twist_ref,
    out_ref,
    lens,
    field,
    target_t,
    rowf,
    acc,
    packed,
    prod,
    send,
    recv,
    gsend,
    grecv,
    send_sem,
    recv_sem,
    gsend_sem,
    grecv_sem,
):
    groups, trials, height, width, kept, chunks = dims
    slim = kept // groups
    part = slim // chunks
    side = 2 * part
    half = groups * part
    span = 2 * kept // chunks
    total = height * groups
    me = lax.axis_index("row")
    mine = lax.axis_index("trial")
    lane_chunks = height // LANES

    barrier = pltpu.get_barrier_semaphore()
    for r in range(1, groups):
        pl.semaphore_signal(
            barrier, inc=1, device_id=(mine, lax.rem(me + r, groups)), device_id_type=MESH
        )
    for r in range(1, trials):
        pl.semaphore_signal(
            barrier, inc=1, device_id=(lax.rem(mine + r, trials), me), device_id_type=MESH
        )

    row_blocks = height // BLK
    col_blocks = width // BLK

    def lens_block(b, carry):
        cb = b // row_blocks
        rb = b % row_blocks
        rows = pl.ds(pl.multiple_of(rb * BLK, BLK), BLK)
        cols = pl.ds(pl.multiple_of(cb * BLK, BLK), BLK)
        offset = level_ref[class_ref[0, rb, cb]]
        where = me * row_blocks + rb
        inside = jnp.where(
            jnp.logical_and(where >= start_ref[cb], where < stop_ref[cb]), 1.0, 0.0
        ).astype(F32)
        angle = phase_ref[rows, cols].T + offset
        cos, sin, whole = turn(angle * (1.0 / math.pi))
        sign = inside - (2.0 * inside) * (whole * whole)
        re = cos * sign
        im = sin * sign
        low = pl.ds(pl.multiple_of(width + cb * BLK, BLK), BLK)
        lens[cols, rows] = re
        lens[low, rows] = im
        field[cols, rows] = re.astype(BF16)
        field[low, rows] = im.astype(BF16)
        return carry

    lax.fori_loop(0, row_blocks * col_blocks, lens_block, 0)

    def copy_to(slot, r):
        to = lax.rem(me + r, groups)
        return pltpu.make_async_remote_copy(
            src_ref=send.at[slot, to],
            dst_ref=recv.at[slot, me],
            send_sem=send_sem.at[slot, r],
            recv_sem=recv_sem.at[slot, r],
            device_id=(mine, to),
            device_id_type=MESH,
        )

    def exchange(slot):
        for r in range(1, groups):
            copy_to(slot, r).start()
        recv[slot, me] = send[slot, me]

    def arrive(slot):
        for r in range(1, groups):
            copy_to(slot, r).wait_recv()

    def columns(slot, q):
        made = jnp.dot(
            fwd_ref[q * span : (q + 1) * span, :], field[...], preferred_element_type=F32
        )
        send[slot] = made.astype(BF16).reshape(groups, side, height)

    def middle(slot_in, slot_out, q, conj):
        arrive(slot_in)

        def mix(n, carry):
            at = pl.ds(pl.multiple_of(n * LANES, LANES), LANES)
            values = []
            for p in range(groups):
                both = recv[slot_in, p, :, at].astype(F32)
                values.append((both[:part], both[part:]))
            for k, (re, im) in enumerate(small_dft(values, -1)):
                t_re = twist_ref[0, k : k + 1, at]
                t_im = twist_ref[1, k : k + 1, at]
                packed[k * part : (k + 1) * part, at] = (re * t_re - im * t_im).astype(BF16)
                packed[half + k * part : half + (k + 1) * part, at] = (
                    re * t_im + im * t_re
                ).astype(BF16)
            return carry

        lax.fori_loop(0, lane_chunks, mix, 0)
        prod[0] = jnp.dot(packed[...], blk_ref[0], preferred_element_type=F32)
        prod[1] = jnp.dot(packed[...], blk_ref[1], preferred_element_type=F32)
        across = (
            lax.broadcasted_iota(jnp.int32, (part, LANES), 0)
            + (me * slim + q * part - kept // 2)
        ).astype(F32)
        c_re, c_im = cos_sin_pi(
            (across * across) * (total / (width * width)) * dist_ref[0]
        )
        c_im = -c_im

        def screen(n, carry):
            at = pl.ds(pl.multiple_of(n * LANES, LANES), LANES)
            for k in range(groups):
                top = slice(k * part, (k + 1) * part)
                low = slice(half + k * part, half + (k + 1) * part)
                s_re = prod[0, top, at] - prod[1, low, at]
                s_im = prod[1, top, at] + prod[0, low, at]
                r_re = rowf[0, k : k + 1, at]
                r_im = rowf[1, k : k + 1, at]
                h_re = r_re * c_re - r_im * c_im
                h_im = r_re * c_im + r_im * c_re
                if conj:
                    h_im = -h_im
                packed[top, at] = (s_re * h_re - s_im * h_im).astype(BF16)
                packed[low, at] = (s_re * h_im + s_im * h_re).astype(BF16)
            return carry

        lax.fori_loop(0, lane_chunks, screen, 0)
        prod[0] = jnp.dot(packed[...], blk_ref[0], preferred_element_type=F32)
        prod[1] = jnp.dot(packed[...], blk_ref[1], preferred_element_type=F32)

        def unmix(n, carry):
            at = pl.ds(pl.multiple_of(n * LANES, LANES), LANES)
            values = []
            for k in range(groups):
                top = slice(k * part, (k + 1) * part)
                low = slice(half + k * part, half + (k + 1) * part)
                u_re = prod[0, top, at] + prod[1, low, at]
                u_im = prod[0, low, at] - prod[1, top, at]
                t_re = twist_ref[0, k : k + 1, at]
                t_im = twist_ref[1, k : k + 1, at]
                values.append(
                    (
                        (u_re * t_re + u_im * t_im).astype(BF16).astype(F32),
                        (u_im * t_re - u_re * t_im).astype(BF16).astype(F32),
                    )
                )
            for p, (re, im) in enumerate(small_dft(values, 1)):
                both = jnp.concatenate([re, im], 0) * (1.0 / total)
                send[slot_out, p, :, at] = both.astype(BF16)
            return carry

        lax.fori_loop(0, lane_chunks, unmix, 0)
        exchange(slot_out)

    def gather_part(slot, q, top):
        near = recv[slot].reshape(span, height)
        return jnp.dot(
            back_ref[pl.ds(top, BLK), q * span : (q + 1) * span],
            near,
            preferred_element_type=F32,
        )

    def spread(first, finish):
        for q in range(chunks - 1):
            arrive(first + q)

            def add(n, carry):
                top = pl.multiple_of(n * BLK, BLK)
                value = gather_part(first + q, q, top)
                at = pl.ds(top, BLK)
                acc[at, :] = value if q == 0 else acc[at, :] + value
                return carry

            lax.fori_loop(0, 2 * col_blocks, add, 0)
        q = chunks - 1
        arrive(first + q)

        def last(n, carry):
            top = pl.multiple_of(n * BLK, BLK)
            low = pl.multiple_of(width + n * BLK, BLK)
            re = gather_part(first + q, q, top)
            im = gather_part(first + q, q, low)
            if chunks > 1:
                re = re + acc[pl.ds(top, BLK), :]
                im = im + acc[pl.ds(low, BLK), :]
            finish(top, low, re * (1.0 / width), im * (1.0 / width))
            return carry

        lax.fori_loop(0, col_blocks, last, 0)

    def weigh(top, low, re, im):
        residual = re * re + im * im - target_t[pl.ds(top, BLK), :]
        field[pl.ds(top, BLK), :] = (residual * re).astype(BF16)
        field[pl.ds(low, BLK), :] = (residual * im).astype(BF16)

    share = width // trials
    per = BLK // share if share < BLK else 1

    def slope(top, low, re, im):
        value = 2.0 * (lens[pl.ds(top, BLK), :] * im - lens[pl.ds(low, BLK), :] * re)
        value = value.astype(BF16)
        if share >= BLK:
            gsend[top // share, pl.ds(pl.multiple_of(top % share, BLK), BLK), :] = value
        else:
            for n in range(per):
                gsend[top // share + n] = value[n * share : (n + 1) * share]

    for q in range(chunks):
        columns(q, q)
        if q == 0:
            pl.semaphore_wait(barrier, groups + trials - 2)
        exchange(q)

    index_k = lax.broadcasted_iota(jnp.int32, (groups, height), 0)
    index_m = lax.broadcasted_iota(jnp.int32, (groups, height), 1)
    freq = index_k + groups * index_m
    signed = jnp.where(freq >= total // 2, freq - total, freq).astype(F32)
    r_cos, r_sin = cos_sin_pi((signed * signed) * (1.0 / total) * dist_ref[0])
    rowf[0] = r_cos
    rowf[1] = -r_sin

    def flip(b, carry):
        rows = pl.ds(pl.multiple_of((b % row_blocks) * BLK, BLK), BLK)
        cols = pl.ds(pl.multiple_of((b // row_blocks) * BLK, BLK), BLK)
        target_t[cols, rows] = target_ref[rows, cols].T
        return carry

    lax.fori_loop(0, row_blocks * col_blocks, flip, 0)

    for q in range(chunks):
        middle(q, chunks + q, q, False)
    spread(chunks, weigh)
    for q in range(chunks):
        columns(2 * chunks + q, q)
        exchange(2 * chunks + q)
    for q in range(chunks):
        middle(2 * chunks + q, 3 * chunks + q, q, True)
    spread(3 * chunks, slope)

    def hand_on(r):
        to = lax.rem(mine + r, trials)
        return pltpu.make_async_remote_copy(
            src_ref=gsend.at[to],
            dst_ref=grecv.at[r],
            send_sem=gsend_sem.at[r],
            recv_sem=grecv_sem.at[r],
            device_id=(to, me),
            device_id_type=MESH,
        )

    for r in range(1, trials):
        hand_on(r).start()
    sum_all = gsend[mine].astype(F32)
    for r in range(1, trials):
        hand_on(r).wait_recv()
        sum_all = sum_all + grecv[r].astype(F32)
    out_ref[...] = sum_all

    for slot in range(4 * chunks):
        for r in range(1, groups):
            copy_to(slot, r).wait_send()
    for r in range(1, trials):
        hand_on(r).wait_send()


def local(phase_map, target, distance, etch_class, class_offset, aperture_start, aperture_stop):
    height, width = phase_map.shape
    kept = width // 2
    groups = lax.axis_size("row")
    trials = lax.axis_size("trial")
    slim = kept // groups
    chunks = 2 if slim % 16 == 0 and slim >= 32 else 1
    side = 2 * slim // chunks
    half = kept // chunks
    share = width // trials
    forward, backward, blk, twist = tables(height, width, kept, groups, chunks)
    import functools

    smem = pl.BlockSpec(memory_space=pltpu.SMEM)
    vmem = pl.BlockSpec(memory_space=pltpu.VMEM)
    out = pl.pallas_call(
        functools.partial(kernel, (groups, trials, height, width, kept, chunks)),
        out_shape=jax.ShapeDtypeStruct((share, height), F32),
        in_specs=[smem] * 5 + [vmem] * 6,
        out_specs=vmem,
        scratch_shapes=[
            pltpu.VMEM((2 * width, height), F32),
            pltpu.VMEM((2 * width, height), BF16),
            pltpu.VMEM((width, height), F32),
            pltpu.VMEM((2, groups, height), F32),
            pltpu.VMEM((2 * width, height), F32),
            pltpu.VMEM((2 * half, height), BF16),
            pltpu.VMEM((2, 2 * half, height), F32),
            pltpu.VMEM((4 * chunks, groups, side, height), BF16),
            pltpu.VMEM((4 * chunks, groups, side, height), BF16),
            pltpu.VMEM((trials, share, height), BF16),
            pltpu.VMEM((trials, share, height), BF16),
            pltpu.SemaphoreType.DMA((4 * chunks, groups)),
            pltpu.SemaphoreType.DMA((4 * chunks, groups)),
            pltpu.SemaphoreType.DMA((trials,)),
            pltpu.SemaphoreType.DMA((trials,)),
        ],
        compiler_params=pltpu.CompilerParams(
            collective_id=0, has_side_effects=True, vmem_limit_bytes=48 * 1024 * 1024
        ),
    )(
        distance,
        etch_class,
        class_offset,
        aperture_start,
        aperture_stop,
        phase_map,
        target,
        forward,
        backward,
        blk,
        twist,
    )
    return out.T


def solution(mesh):
    return jax.shard_map(
        local,
        mesh=mesh,
        in_specs=(
            P("row", None),
            P("row", None),
            P("trial"),
            P("trial", "row", None),
            P(),
            P(),
            P(),
        ),
        out_specs=P("row", "trial"),
        check_vma=False,
    )
```

time: 172 us -> 60.1 us (0.35)
  Pallas kernels: 0 us -> 50.6 us
  waiting for transfers between devices: 50.6 us -> 0 us
  other arithmetic: 39.1 us -> 0 us
  starting transfers between devices: 24.6 us -> 0 us
  blocking collectives: 18.6 us -> 0 us
  matrix products: 15.7 us -> 0 us
  between operations: 14.6 us -> 0.74 us
    pallas_call x0 -> x1, Pallas kernels: none -> 50.6 us  [local(): pl.pallas_call(functools.partial(kernel, (groups, trials, height, width,...]
    all_to_all x6 -> x0, waiting for transfers between devices: 29.2 us -> none  [the longest x2 12.5 us: forward_columns(): lax.all_to_all(cols_imag, 'row', split_axis=0, concat_axis=1, tiled=True)]
    convert_element_type x12 -> x0, other arithmetic: 29.2 us -> none  [the longest x2 5.29 us: column_tables(): table_imag = table_imag.astype(jnp.bfloat16)]
    all_to_all x6 -> x0, starting transfers between devices: 24.6 us -> none  [the longest x2 8.1 us: inverse_columns(): lax.all_to_all(near_real, 'row', split_axis=1, concat_axis=0, tiled=True)]
    unnamed x2 -> x0, waiting for transfers between devices: 21.4 us -> none
    all_to_all x2 -> x0, blocking collectives: 18.6 us -> none  [the longest x1 9.3 us: inverse_columns(): lax.all_to_all(near_imag, 'row', split_axis=1, concat_axis=0, tiled=True)]
    dot_general x24 -> x0, matrix products: 15.7 us -> none  [the longest x16 7.7 us: small_einsum(): return jnp.einsum(form, table, values, precision=HIGHEST_PRECISION)]
    neg x3 -> x0, other arithmetic: 8.81 us -> none  [the longest x1 4.64 us: block_tables(): -table_imag]
  transfers between devices with their start and end apart: 7 -> 0, of which waited for: 6 -> 0; matrix products, arithmetic and copies ran while one was open for 13% -> 0% of each run, Pallas kernels for 0% -> 0%
where the time goes in v1:
time: 60.1 us; the launch traced here: 59.7 us
  Pallas kernels  50.6 us (84%)
  local copies, waits for them, and re-layouts  8.4 us (14%)
  between operations  0.74 us (1%)
    pallas_call x1, Pallas kernels, local(): pl.pallas_call(functools.partial(kernel, (groups, trials, height, width,...  50.6 us
    unnamed x20, local copies, waits for them, and re-layouts  7.56 us

profile of v1, /device:TPU:0, one launch (start us, length us, event | category | flops | bytes accessed | tf_op | source)
XLA Modules:
  0.0 59.7 jit_solution(7597230456204590911)
XLA Ops:
  0.0 0.0 copy-start.9
  0.0 0.0 copy-start.8
  0.0 0.0 copy-start.7
  0.7 0.0 copy-done.9
  0.7 0.0 copy-done.8
  0.7 0.0 copy-done.7
  0.7 0.0 copy-start
  0.7 1.2 %copy-done = f32[512,512]{1,0:T(8,128)S(1)} copy-done((f32[512,512]{1,0:T(8,128)S(1)}, f32[512,512]{1,0:T(8,128)}, u32[]{:S(2)}) %copy-start) | copy-done | bytes 1048600
  2.0 0.0 copy-start.1
  2.0 1.2 %copy-done.1 = f32[512,512]{1,0:T(8,128)S(1)} copy-done((f32[512,512]{1,0:T(8,128)S(1)}, f32[512,512]{1,0:T(8,128)}, u32[]{:S(2)}) %copy-start.1) | copy-done | bytes 1048600
  3.2 0.0 copy-start.2
  3.2 1.2 %copy-done.2 = bf16[2,512,512]{2,1,0:T(8,128)(2,1)S(1)} copy-done((bf16[2,512,512]{2,1,0:T(8,128)(2,1)S(1)}, bf16[2,512,512]{2,1,0:T(8,128)(2,1)}, u32[]{:S(2)}) %copy-start.2) | copy-done | bytes 1048600
  4.4 0.0 copy-start.3
  4.4 1.2 %copy-done.3 = bf16[1024,512]{1,0:T(8,128)(2,1)S(1)} copy-done((bf16[1024,512]{1,0:T(8,128)(2,1)S(1)}, bf16[1024,512]{1,0:T(8,128)(2,1)}, u32[]{:S(2)}) %copy-start.3) | copy-done | bytes 1048600
  5.6 0.0 copy-start.4
  5.6 1.2 %copy-done.4 = bf16[512,1024]{1,0:T(8,128)(2,1)S(1)} copy-done((bf16[512,1024]{1,0:T(8,128)(2,1)S(1)}, bf16[512,1024]{1,0:T(8,128)(2,1)}, u32[]{:S(2)}) %copy-start.4) | copy-done | bytes 1048600
  6.9 0.0 copy-start.5
  6.9 0.8 %copy-done.5 = f32[2,8,512]{2,1,0:T(8,128)S(1)} copy-done((f32[2,8,512]{2,1,0:T(8,128)S(1)}, f32[2,8,512]{2,1,0:T(8,128)}, u32[]{:S(2)}) %copy-start.5) | copy-done | bytes 32792
  7.6 0.0 copy-start.6
  7.6 0.7 %copy-done.6 = s32[1,4,4]{2,1,0:T(4,128)S(1)} copy-done((s32[1,4,4]{2,1,0:T(4,128)S(1)}, s32[1,4,4]{2,1,0:T(4,128)}, u32[]{:S(2)}) %copy-start.6) | copy-done | bytes 88
  8.3 50.6 %shard_map.109 = f32[128,512]{1,0:T(8,128)S(1)} custom-call(f32[1]{0:T(128)S(6)} %copy.13.dist_ref, s32[1,4,4]{2,1,0:T(4,128)S(1)} %copy-done.6, f32[4]{0:T(128)S(1)} %copy-done.7, s32[4]{0:T(128)S(1)} %copy-done.8, s32[4]{0:T(128)S(1)} %copy-done.9, f32[512,512]{1,0:T(8,128)S(1)} %copy-done, f32[512,512]{1,0:T(8,128)S(1)} %copy-done.1, ...), custom_call_target="tpu_custom_call" | custom-call | tf_op jit(solution)/shard_map/pallas_call | solution.py:407
  58.9 0.8 %copy.12 = f32[512,128]{1,0:T(8,128)} copy(f32[512,128]{0,1:T(8,128)S(1)} %bitcast.1) | data formatting | bytes 524288 | tf_op jit(solution)/shard_map/transpose | solution.py:445
Async XLA Ops:
  0.0 0.7 %copy-start.9 = (s32[4]{0:T(128)S(1)}, s32[4]{0:T(128)}, u32[]{:S(2)}) copy-start(s32[4]{0:T(128)} %stop_ref.1) | copy-start | bytes 52
  0.0 0.7 %copy-start.8 = (s32[4]{0:T(128)S(1)}, s32[4]{0:T(128)}, u32[]{:S(2)}) copy-start(s32[4]{0:T(128)} %start_ref.1) | copy-start | bytes 52
  0.0 0.7 %copy-start.7 = (f32[4]{0:T(128)S(1)}, f32[4]{0:T(128)}, u32[]{:S(2)}) copy-start(f32[4]{0:T(128)} %level_ref.1) | copy-start | bytes 52
  0.7 1.2 %copy-start = (f32[512,512]{1,0:T(8,128)S(1)}, f32[512,512]{1,0:T(8,128)}, u32[]{:S(2)}) copy-start(f32[512,512]{1,0:T(8,128)} %phase_ref.1) | copy-start | bytes 3145732
  2.0 1.2 %copy-start.1 = (f32[512,512]{1,0:T(8,128)S(1)}, f32[512,512]{1,0:T(8,128)}, u32[]{:S(2)}) copy-start(f32[512,512]{1,0:T(8,128)} %target_ref.1) | copy-start | bytes 3145732
  3.2 1.2 %copy-start.2 = (bf16[2,512,512]{2,1,0:T(8,128)(2,1)S(1)}, bf16[2,512,512]{2,1,0:T(8,128)(2,1)}, u32[]{:S(2)}) copy-start(bf16[2,512,512]{2,1,0:T(8,128)(2,1)} %constant.10.clone.blk_ref) | copy-start | bytes 3145732
  4.4 1.2 %copy-start.3 = (bf16[1024,512]{1,0:T(8,128)(2,1)S(1)}, bf16[1024,512]{1,0:T(8,128)(2,1)}, u32[]{:S(2)}) copy-start(bf16[1024,512]{1,0:T(8,128)(2,1)} %constant.9.clone.back_ref) | copy-start | bytes 3145732
  5.6 1.2 %copy-start.4 = (bf16[512,1024]{1,0:T(8,128)(2,1)S(1)}, bf16[512,1024]{1,0:T(8,128)(2,1)}, u32[]{:S(2)}) copy-start(bf16[512,1024]{1,0:T(8,128)(2,1)} %constant.8.clone.fwd_ref) | copy-start | bytes 3145732
  6.9 0.8 %copy-start.5 = (f32[2,8,512]{2,1,0:T(8,128)S(1)}, f32[2,8,512]{2,1,0:T(8,128)}, u32[]{:S(2)}) copy-start(f32[2,8,512]{2,1,0:T(8,128)} %constant.11.clone.twist_ref) | copy-start | bytes 98308
  7.6 0.7 %copy-start.6 = (s32[1,4,4]{2,1,0:T(4,128)S(1)}, s32[1,4,4]{2,1,0:T(4,128)}, u32[]{:S(2)}) copy-start(s32[1,4,4]{2,1,0:T(4,128)} %class_ref.1) | copy-start | bytes 196

commit v2 on v1

--- a/solution.py
+++ b/solution.py
@@ -1,3 +1,4 @@
+import functools
 import math
 
 import jax
@@ -106,13 +107,20 @@
     level_ref,
     start_ref,
     stop_ref,
+    phase_hbm,
+    target_hbm,
+    fwd_hbm,
+    back_hbm,
+    blk_hbm,
+    twist_hbm,
+    out_ref,
     phase_ref,
     target_ref,
     fwd_ref,
     back_ref,
     blk_ref,
     twist_ref,
-    out_ref,
+    fetch_sem,
     lens,
     field,
     target_t,
@@ -140,6 +148,31 @@
     mine = lax.axis_index("trial")
     lane_chunks = height // LANES
 
+    fetches = {}
+
+    def fetch(name, source, dest, pieces):
+        rows = source.shape[0] // pieces
+        made = []
+        for n in range(pieces):
+            at = pl.ds(n * rows, rows)
+            place = sum(len(c) for c in fetches.values()) + n
+            made.append(
+                pltpu.make_async_copy(source.at[at], dest.at[at], fetch_sem.at[place])
+            )
+            made[-1].start()
+        fetches[name] = made
+
+    def fetched(name):
+        for made in fetches[name]:
+            made.wait()
+
+    fetch("phase", phase_hbm, phase_ref, height // BLK)
+    fetch("fwd", fwd_hbm, fwd_ref, 4)
+    fetch("twist", twist_hbm, twist_ref, 1)
+    fetch("target", target_hbm, target_ref, 4)
+    fetch("blk", blk_hbm, blk_ref, 2)
+    fetch("back", back_hbm, back_ref, 4)
+
     barrier = pltpu.get_barrier_semaphore()
     for r in range(1, groups):
         pl.semaphore_signal(
@@ -153,10 +186,8 @@
     row_blocks = height // BLK
     col_blocks = width // BLK
 
-    def lens_block(b, carry):
-        cb = b // row_blocks
-        rb = b % row_blocks
-        rows = pl.ds(pl.multiple_of(rb * BLK, BLK), BLK)
+    def lens_block(rb, cb, carry):
+        rows = pl.ds(rb * BLK, BLK)
         cols = pl.ds(pl.multiple_of(cb * BLK, BLK), BLK)
         offset = level_ref[class_ref[0, rb, cb]]
         where = me * row_blocks + rb
@@ -175,7 +206,9 @@
         field[low, rows] = im.astype(BF16)
         return carry
 
-    lax.fori_loop(0, row_blocks * col_blocks, lens_block, 0)
+    for rb in range(row_blocks):
+        fetches["phase"][rb].wait()
+        lax.fori_loop(0, col_blocks, functools.partial(lens_block, rb), 0)
 
     def copy_to(slot, r):
         to = lax.rem(me + r, groups)
@@ -278,15 +311,15 @@
         lax.fori_loop(0, lane_chunks, unmix, 0)
         exchange(slot_out)
 
-    def gather_part(slot, q, top):
+    def gather_part(slot, q, top, block=BLK):
         near = recv[slot].reshape(span, height)
         return jnp.dot(
-            back_ref[pl.ds(top, BLK), q * span : (q + 1) * span],
+            back_ref[pl.ds(top, block), q * span : (q + 1) * span],
             near,
             preferred_element_type=F32,
         )
 
-    def spread(first, finish):
+    def spread(first, block, finish):
         for q in range(chunks - 1):
             arrive(first + q)
 
@@ -301,67 +334,26 @@
         q = chunks - 1
         arrive(first + q)
 
-        def last(n, carry):
-            top = pl.multiple_of(n * BLK, BLK)
-            low = pl.multiple_of(width + n * BLK, BLK)
-            re = gather_part(first + q, q, top)
-            im = gather_part(first + q, q, low)
-            if chunks > 1:
-                re = re + acc[pl.ds(top, BLK), :]
-                im = im + acc[pl.ds(low, BLK), :]
-            finish(top, low, re * (1.0 / width), im * (1.0 / width))
-            return carry
-
-        lax.fori_loop(0, col_blocks, last, 0)
-
-    def weigh(top, low, re, im):
-        residual = re * re + im * im - target_t[pl.ds(top, BLK), :]
-        field[pl.ds(top, BLK), :] = (residual * re).astype(BF16)
-        field[pl.ds(low, BLK), :] = (residual * im).astype(BF16)
+        for n in range(width // block):
+            finish(n, functools.partial(result, first + q, q, block))
+
+    def result(slot, q, block, n):
+        top = pl.multiple_of(n * block, block)
+        low = pl.multiple_of(width + n * block, block)
+        re = gather_part(slot, q, top, block)
+        im = gather_part(slot, q, low, block)
+        if chunks > 1:
+            re = re + acc[pl.ds(top, block), :]
+            im = im + acc[pl.ds(low, block), :]
+        return pl.ds(top, block), pl.ds(low, block), re * (1.0 / width), im * (1.0 / width)
+
+    def weigh(n, made):
+        top, low, re, im = made(n)
+        residual = re * re + im * im - target_t[top, :]
+        field[top, :] = (residual * re).astype(BF16)
+        field[low, :] = (residual * im).astype(BF16)
 
     share = width // trials
-    per = BLK // share if share < BLK else 1
-
-    def slope(top, low, re, im):
-        value = 2.0 * (lens[pl.ds(top, BLK), :] * im - lens[pl.ds(low, BLK), :] * re)
-        value = value.astype(BF16)
-        if share >= BLK:
-            gsend[top // share, pl.ds(pl.multiple_of(top % share, BLK), BLK), :] = value
-        else:
-            for n in range(per):
-                gsend[top // share + n] = value[n * share : (n + 1) * share]
-
-    for q in range(chunks):
-        columns(q, q)
-        if q == 0:
-            pl.semaphore_wait(barrier, groups + trials - 2)
-        exchange(q)
-
-    index_k = lax.broadcasted_iota(jnp.int32, (groups, height), 0)
-    index_m = lax.broadcasted_iota(jnp.int32, (groups, height), 1)
-    freq = index_k + groups * index_m
-    signed = jnp.where(freq >= total // 2, freq - total, freq).astype(F32)
-    r_cos, r_sin = cos_sin_pi((signed * signed) * (1.0 / total) * dist_ref[0])
-    rowf[0] = r_cos
-    rowf[1] = -r_sin
-
-    def flip(b, carry):
-        rows = pl.ds(pl.multiple_of((b % row_blocks) * BLK, BLK), BLK)
-        cols = pl.ds(pl.multiple_of((b // row_blocks) * BLK, BLK), BLK)
-        target_t[cols, rows] = target_ref[rows, cols].T
-        return carry
-
-    lax.fori_loop(0, row_blocks * col_blocks, flip, 0)
-
-    for q in range(chunks):
-        middle(q, chunks + q, q, False)
-    spread(chunks, weigh)
-    for q in range(chunks):
-        columns(2 * chunks + q, q)
-        exchange(2 * chunks + q)
-    for q in range(chunks):
-        middle(2 * chunks + q, 3 * chunks + q, q, True)
-    spread(3 * chunks, slope)
 
     def hand_on(r):
         to = lax.rem(mine + r, trials)
@@ -374,8 +366,53 @@
             device_id_type=MESH,
         )
 
-    for r in range(1, trials):
-        hand_on(r).start()
+    def slope(n, made):
+        r = (n + 1) % trials
+        to = lax.rem(mine + r, trials)
+        top, low, re, im = made(to)
+        value = 2.0 * (lens[top, :] * im - lens[low, :] * re)
+        gsend[to] = value.astype(BF16)
+        if r:
+            hand_on(r).start()
+
+    fetched("fwd")
+    for q in range(chunks):
+        columns(q, q)
+        if q == 0:
+            pl.semaphore_wait(barrier, groups + trials - 2)
+        exchange(q)
+
+    index_k = lax.broadcasted_iota(jnp.int32, (groups, height), 0)
+    index_m = lax.broadcasted_iota(jnp.int32, (groups, height), 1)
+    freq = index_k + groups * index_m
+    signed = jnp.where(freq >= total // 2, freq - total, freq).astype(F32)
+    r_cos, r_sin = cos_sin_pi((signed * signed) * (1.0 / total) * dist_ref[0])
+    rowf[0] = r_cos
+    rowf[1] = -r_sin
+
+    def flip(b, carry):
+        rows = pl.ds(pl.multiple_of((b % row_blocks) * BLK, BLK), BLK)
+        cols = pl.ds(pl.multiple_of((b // row_blocks) * BLK, BLK), BLK)
+        target_t[cols, rows] = target_ref[rows, cols].T
+        return carry
+
+    fetched("target")
+    lax.fori_loop(0, row_blocks * col_blocks, flip, 0)
+    fetched("twist")
+    fetched("blk")
+
+    for q in range(chunks):
+        middle(q, chunks + q, q, False)
+        if q == 0:
+            fetched("back")
+    spread(chunks, BLK, weigh)
+    for q in range(chunks):
+        columns(2 * chunks + q, q)
+        exchange(2 * chunks + q)
+    for q in range(chunks):
+        middle(2 * chunks + q, 3 * chunks + q, q, True)
+    spread(3 * chunks, share, slope)
+
     sum_all = gsend[mine].astype(F32)
     for r in range(1, trials):
         hand_on(r).wait_recv()
@@ -400,16 +437,22 @@
     half = kept // chunks
     share = width // trials
     forward, backward, blk, twist = tables(height, width, kept, groups, chunks)
-    import functools
-
     smem = pl.BlockSpec(memory_space=pltpu.SMEM)
+    hbm = pl.BlockSpec(memory_space=pltpu.HBM)
     vmem = pl.BlockSpec(memory_space=pltpu.VMEM)
     out = pl.pallas_call(
         functools.partial(kernel, (groups, trials, height, width, kept, chunks)),
         out_shape=jax.ShapeDtypeStruct((share, height), F32),
-        in_specs=[smem] * 5 + [vmem] * 6,
+        in_specs=[smem] * 5 + [hbm] * 6,
         out_specs=vmem,
         scratch_shapes=[
+            pltpu.VMEM(phase_map.shape, F32),
+            pltpu.VMEM(target.shape, F32),
+            pltpu.VMEM(forward.shape, BF16),
+            pltpu.VMEM(backward.shape, BF16),
+            pltpu.VMEM(blk.shape, BF16),
+            pltpu.VMEM(twist.shape, F32),
+            pltpu.SemaphoreType.DMA((height // BLK + 15,)),
             pltpu.VMEM((2 * width, height), F32),
             pltpu.VMEM((2 * width, height), BF16),
             pltpu.VMEM((width, height), F32),

time: 60.1 us -> 59.6 us (level)
  no operation moved by 1% of the time
where the time goes in v2:
time: 59.6 us; the launch traced here: 59.2 us
  Pallas kernels  50 us (84%)
  local copies, waits for them, and re-layouts  8.4 us (14%)
  between operations  0.74 us (1%)
    pallas_call x1, Pallas kernels, local(): pl.pallas_call(functools.partial(kernel, (groups, trials, height, width,...  50 us
    unnamed x20, local copies, waits for them, and re-layouts  7.56 us

profile of v2, /device:TPU:0, one launch (start us, length us, event | category | flops | bytes accessed | tf_op | source)
XLA Modules:
  0.0 59.2 jit_solution(17598966063391714697)
XLA Ops:
  0.0 0.0 copy-start.9
  0.0 0.0 copy-start.8
  0.0 0.0 copy-start.7
  0.7 0.0 copy-done.9
  0.7 0.0 copy-done.8
  0.7 0.0 copy-done.7
  0.7 0.0 copy-start
  0.7 1.2 %copy-done = f32[512,512]{1,0:T(8,128)S(1)} copy-done((f32[512,512]{1,0:T(8,128)S(1)}, f32[512,512]{1,0:T(8,128)}, u32[]{:S(2)}) %copy-start) | copy-done | bytes 1048600
  2.0 0.0 copy-start.1
  2.0 1.2 %copy-done.1 = f32[512,512]{1,0:T(8,128)S(1)} copy-done((f32[512,512]{1,0:T(8,128)S(1)}, f32[512,512]{1,0:T(8,128)}, u32[]{:S(2)}) %copy-start.1) | copy-done | bytes 1048600
  3.2 0.0 copy-start.2
  3.2 1.2 %copy-done.2 = bf16[2,512,512]{2,1,0:T(8,128)(2,1)S(1)} copy-done((bf16[2,512,512]{2,1,0:T(8,128)(2,1)S(1)}, bf16[2,512,512]{2,1,0:T(8,128)(2,1)}, u32[]{:S(2)}) %copy-start.2) | copy-done | bytes 1048600
  4.4 0.0 copy-start.3
  4.4 1.2 %copy-done.3 = bf16[1024,512]{1,0:T(8,128)(2,1)S(1)} copy-done((bf16[1024,512]{1,0:T(8,128)(2,1)S(1)}, bf16[1024,512]{1,0:T(8,128)(2,1)}, u32[]{:S(2)}) %copy-start.3) | copy-done | bytes 1048600
  5.6 0.0 copy-start.4
  5.6 1.2 %copy-done.4 = bf16[512,1024]{1,0:T(8,128)(2,1)S(1)} copy-done((bf16[512,1024]{1,0:T(8,128)(2,1)S(1)}, bf16[512,1024]{1,0:T(8,128)(2,1)}, u32[]{:S(2)}) %copy-start.4) | copy-done | bytes 1048600
  6.9 0.0 copy-start.5
  6.9 0.8 %copy-done.5 = f32[2,8,512]{2,1,0:T(8,128)S(1)} copy-done((f32[2,8,512]{2,1,0:T(8,128)S(1)}, f32[2,8,512]{2,1,0:T(8,128)}, u32[]{:S(2)}) %copy-start.5) | copy-done | bytes 32792
  7.6 0.0 copy-start.6
  7.6 0.7 %copy-done.6 = s32[1,4,4]{2,1,0:T(4,128)S(1)} copy-done((s32[1,4,4]{2,1,0:T(4,128)S(1)}, s32[1,4,4]{2,1,0:T(4,128)}, u32[]{:S(2)}) %copy-start.6) | copy-done | bytes 88
  8.3 50.0 %shard_map.109 = f32[128,512]{1,0:T(8,128)S(1)} custom-call(f32[1]{0:T(128)S(6)} %copy.13.dist_ref, s32[1,4,4]{2,1,0:T(4,128)S(1)} %copy-done.6, f32[4]{0:T(128)S(1)} %copy-done.7, s32[4]{0:T(128)S(1)} %copy-done.8, s32[4]{0:T(128)S(1)} %copy-done.9, f32[512,512]{1,0:T(8,128)S(1)} %copy-done, f32[512,512]{1,0:T(8,128)S(1)} %copy-done.1, ...), custom_call_target="tpu_custom_call" | custom-call | tf_op jit(solution)/shard_map/pallas_call | solution.py:443
  58.3 0.8 %copy.12 = f32[512,128]{1,0:T(8,128)} copy(f32[512,128]{0,1:T(8,128)S(1)} %bitcast.1) | data formatting | bytes 524288 | tf_op jit(solution)/shard_map/transpose | solution.py:488
Async XLA Ops:
  0.0 0.7 %copy-start.9 = (s32[4]{0:T(128)S(1)}, s32[4]{0:T(128)}, u32[]{:S(2)}) copy-start(s32[4]{0:T(128)} %stop_ref.1) | copy-start | bytes 52
  0.0 0.7 %copy-start.8 = (s32[4]{0:T(128)S(1)}, s32[4]{0:T(128)}, u32[]{:S(2)}) copy-start(s32[4]{0:T(128)} %start_ref.1) | copy-start | bytes 52
  0.0 0.7 %copy-start.7 = (f32[4]{0:T(128)S(1)}, f32[4]{0:T(128)}, u32[]{:S(2)}) copy-start(f32[4]{0:T(128)} %level_ref.1) | copy-start | bytes 52
  0.7 1.2 %copy-start = (f32[512,512]{1,0:T(8,128)S(1)}, f32[512,512]{1,0:T(8,128)}, u32[]{:S(2)}) copy-start(f32[512,512]{1,0:T(8,128)} %phase_hbm.1) | copy-start | bytes 3145732
  2.0 1.2 %copy-start.1 = (f32[512,512]{1,0:T(8,128)S(1)}, f32[512,512]{1,0:T(8,128)}, u32[]{:S(2)}) copy-start(f32[512,512]{1,0:T(8,128)} %target_hbm.1) | copy-start | bytes 3145732
  3.2 1.2 %copy-start.2 = (bf16[2,512,512]{2,1,0:T(8,128)(2,1)S(1)}, bf16[2,512,512]{2,1,0:T(8,128)(2,1)}, u32[]{:S(2)}) copy-start(bf16[2,512,512]{2,1,0:T(8,128)(2,1)} %constant.10.clone.blk_hbm) | copy-start | bytes 3145732
  4.4 1.2 %copy-start.3 = (bf16[1024,512]{1,0:T(8,128)(2,1)S(1)}, bf16[1024,512]{1,0:T(8,128)(2,1)}, u32[]{:S(2)}) copy-start(bf16[1024,512]{1,0:T(8,128)(2,1)} %constant.9.clone.back_hbm) | copy-start | bytes 3145732
  5.6 1.2 %copy-start.4 = (bf16[512,1024]{1,0:T(8,128)(2,1)S(1)}, bf16[512,1024]{1,0:T(8,128)(2,1)}, u32[]{:S(2)}) copy-start(bf16[512,1024]{1,0:T(8,128)(2,1)} %constant.8.clone.fwd_hbm) | copy-start | bytes 3145732
  6.9 0.8 %copy-start.5 = (f32[2,8,512]{2,1,0:T(8,128)S(1)}, f32[2,8,512]{2,1,0:T(8,128)}, u32[]{:S(2)}) copy-start(f32[2,8,512]{2,1,0:T(8,128)} %constant.11.clone.twist_hbm) | copy-start | bytes 98308
  7.6 0.7 %copy-start.6 = (s32[1,4,4]{2,1,0:T(4,128)S(1)}, s32[1,4,4]{2,1,0:T(4,128)}, u32[]{:S(2)}) copy-start(s32[1,4,4]{2,1,0:T(4,128)} %class_ref.1) | copy-start | bytes 196

commit v3 on v2

--- a/solution.py
+++ b/solution.py
@@ -470,7 +470,7 @@
             pltpu.SemaphoreType.DMA((trials,)),
         ],
         compiler_params=pltpu.CompilerParams(
-            collective_id=0, has_side_effects=True, vmem_limit_bytes=48 * 1024 * 1024
+            collective_id=0, has_side_effects=True, vmem_limit_bytes=67_043_328
         ),
     )(
         distance,

time: 59.6 us -> 54 us (0.906)
  local copies, waits for them, and re-layouts: 8.4 us -> 1.79 us
  Pallas kernels: 50 us -> 51.3 us
    unnamed x20 -> x0, local copies, waits for them, and re-layouts: 7.56 us -> none
    pallas_call x1, Pallas kernels: 50 us -> 51.3 us  [local(): pl.pallas_call(functools.partial(kernel, (groups, trials, height, width,...]
    transpose x1, local copies, waits for them, and re-layouts: 0.84 us -> 1.79 us  [local(): return out.T]
where the time goes in v3:
time: 54 us; the launch traced here: 53.7 us
  Pallas kernels  51.3 us (95%)
  local copies, waits for them, and re-layouts  1.79 us (3%)
  between operations  0.66 us (1%)
    pallas_call x1, Pallas kernels, local(): pl.pallas_call(functools.partial(kernel, (groups, trials, height, width,...  51.3 us
    transpose x1, local copies, waits for them, and re-layouts, local(): return out.T  1.79 us

profile of v3, /device:TPU:0, one launch (start us, length us, event | category | flops | bytes accessed | tf_op | source)
XLA Modules:
  0.0 53.7 jit_solution(5348452761383343276)
XLA Ops:
  0.7 51.3 %shard_map.109 = f32[128,512]{1,0:T(8,128)} custom-call(f32[1]{0:T(128)S(6)} %copy.13.dist_ref, s32[1,4,4]{2,1,0:T(4,128)} %class_ref.1, f32[4]{0:T(128)} %level_ref.1, s32[4]{0:T(128)} %start_ref.1, s32[4]{0:T(128)} %stop_ref.1, f32[512,512]{1,0:T(8,128)} %phase_hbm.1, f32[512,512]{1,0:T(8,128)} %target_hbm.1, bf16[512,1024]{1,0:T(8,128)(2,1)} %constant.8.clone.fwd_hbm, ...), custom_call_target="tpu_custom_call" | custom-call | tf_op jit(solution)/shard_map/pallas_call | solution.py:443
  52.0 1.8 %copy.12 = f32[512,128]{1,0:T(8,128)} copy(f32[512,128]{0,1:T(8,128)} %bitcast.1) | data formatting | bytes 524288 | tf_op jit(solution)/shard_map/transpose | solution.py:488

commit v4 on v3

--- a/solution.py
+++ b/solution.py
@@ -168,10 +168,6 @@
 
     fetch("phase", phase_hbm, phase_ref, height // BLK)
     fetch("fwd", fwd_hbm, fwd_ref, 4)
-    fetch("twist", twist_hbm, twist_ref, 1)
-    fetch("target", target_hbm, target_ref, 4)
-    fetch("blk", blk_hbm, blk_ref, 2)
-    fetch("back", back_hbm, back_ref, 4)
 
     barrier = pltpu.get_barrier_semaphore()
     for r in range(1, groups):
@@ -376,6 +372,10 @@
             hand_on(r).start()
 
     fetched("fwd")
+    fetch("twist", twist_hbm, twist_ref, 1)
+    fetch("target", target_hbm, target_ref, 4)
+    fetch("blk", blk_hbm, blk_ref, 2)
+    fetch("back", back_hbm, back_ref, 4)
     for q in range(chunks):
         columns(q, q)
         if q == 0:

time: 54 us -> 54 us (level)
  no operation moved by 1% of the time
where the time goes in v4:
time: 54 us; the launch traced here: 53.8 us
  Pallas kernels  51.3 us (95%)
  local copies, waits for them, and re-layouts  1.79 us (3%)
  between operations  0.66 us (1%)
    pallas_call x1, Pallas kernels, local(): pl.pallas_call(functools.partial(kernel, (groups, trials, height, width,...  51.3 us
    transpose x1, local copies, waits for them, and re-layouts, local(): return out.T  1.79 us

profile of v4, /device:TPU:0, one launch (start us, length us, event | category | flops | bytes accessed | tf_op | source)
XLA Modules:
  0.0 53.8 jit_solution(4447799454699701488)
XLA Ops:
  0.7 51.3 %shard_map.109 = f32[128,512]{1,0:T(8,128)} custom-call(f32[1]{0:T(128)S(6)} %copy.13.dist_ref, s32[1,4,4]{2,1,0:T(4,128)} %class_ref.1, f32[4]{0:T(128)} %level_ref.1, s32[4]{0:T(128)} %start_ref.1, s32[4]{0:T(128)} %stop_ref.1, f32[512,512]{1,0:T(8,128)} %phase_hbm.1, f32[512,512]{1,0:T(8,128)} %target_hbm.1, bf16[512,1024]{1,0:T(8,128)(2,1)} %constant.8.clone.fwd_hbm, ...), custom_call_target="tpu_custom_call" | custom-call | tf_op jit(solution)/shard_map/pallas_call | solution.py:443
  52.0 1.8 %copy.12 = f32[512,128]{1,0:T(8,128)} copy(f32[512,128]{0,1:T(8,128)} %bitcast.1) | data formatting | bytes 524288 | tf_op jit(solution)/shard_map/transpose | solution.py:488

commit v5 on v4

--- a/solution.py
+++ b/solution.py
@@ -218,7 +218,7 @@
         )
 
     def exchange(slot):
-        for r in range(1, groups):
+        for r in sorted(range(1, groups), key=lambda r: min(r, groups - r)):
             copy_to(slot, r).start()
         recv[slot, me] = send[slot, me]
 

time: 54 us -> 54.9 us (1.017)
  Pallas kernels: 51.3 us -> 52.2 us
    pallas_call x1, Pallas kernels: 51.3 us -> 52.2 us  [local(): pl.pallas_call(functools.partial(kernel, (groups, trials, height, width,...]
where the time goes in v5:
time: 54.9 us; the launch traced here: 54.7 us
  Pallas kernels  52.2 us (95%)
  local copies, waits for them, and re-layouts  1.79 us (3%)
  between operations  0.66 us (1%)
    pallas_call x1, Pallas kernels, local(): pl.pallas_call(functools.partial(kernel, (groups, trials, height, width,...  52.2 us
    transpose x1, local copies, waits for them, and re-layouts, local(): return out.T  1.79 us

profile of v5, /device:TPU:0, one launch (start us, length us, event | category | flops | bytes accessed | tf_op | source)
XLA Modules:
  0.0 54.7 jit_solution(4661288147370658826)
XLA Ops:
  0.7 52.2 %shard_map.109 = f32[128,512]{1,0:T(8,128)} custom-call(f32[1]{0:T(128)S(6)} %copy.13.dist_ref, s32[1,4,4]{2,1,0:T(4,128)} %class_ref.1, f32[4]{0:T(128)} %level_ref.1, s32[4]{0:T(128)} %start_ref.1, s32[4]{0:T(128)} %stop_ref.1, f32[512,512]{1,0:T(8,128)} %phase_hbm.1, f32[512,512]{1,0:T(8,128)} %target_hbm.1, bf16[512,1024]{1,0:T(8,128)(2,1)} %constant.8.clone.fwd_hbm, ...), custom_call_target="tpu_custom_call" | custom-call | tf_op jit(solution)/shard_map/pallas_call | solution.py:443
  52.9 1.8 %copy.12 = f32[512,128]{1,0:T(8,128)} copy(f32[512,128]{0,1:T(8,128)} %bitcast.1) | data formatting | bytes 524288 | tf_op jit(solution)/shard_map/transpose | solution.py:488
